TPU v7x, 32 devices: a whole 2x2x4 slice. The times are simulated.
32 devices in a mesh: dp: 8 (over y, x, core), tensor: 4 (over z).
Axes of the slice: x: 2, y: 2, z: 4, core: 2. Of those that a mesh axis runs over, the one named last changes fastest.
Arguments:
- inputs: bfloat16 [6144, 2048], P('dp'), may hold values from -6 to 6
- block_ids: int32 [8, 768], P('dp'), may hold values from 0 to 3, never falling along the last dimension, each value on 1 to 256 neighbouring positions
- first_gain: float32 [2048], replicated, may hold values from 0.5 to 1.5
- first_shift: float32 [2048], replicated, may hold values from -3 to 3
- mixing_weight: bfloat16 [2048, 3, 2048], P(None, None, 'tensor'), may hold values from -0.125 to 0.125
- mixing_bias: float32 [2, 2048], P(None, 'tensor'), may hold values from -3 to 3
- output_weight: bfloat16 [2048, 2048], P('tensor'), may hold values from -0.75 to 0.75
- output_bias: float32 [2048], replicated, may hold values from -3 to 3
- second_gain: float32 [2048], replicated, may hold values from 0.5 to 1.5
- second_shift: float32 [2048], replicated, may hold values from -3 to 3
- expand_weight: bfloat16 [2048, 8192], P(None, 'tensor'), may hold values from -0.125 to 0.125
- expand_bias: float32 [8192], P('tensor'), may hold values from -3 to 3
- shrink_weight: bfloat16 [8192, 2048], P('tensor'), may hold values from -0.0625 to 0.0625
- shrink_bias: float32 [2048], replicated, may hold values from -3 to 3
- cotangent: bfloat16 [6144, 2048], P('dp'), may hold values from -6 to 6
Outputs:
- outputs: bfloat16 [6144, 2048], P('dp')
- input_grad: bfloat16 [6144, 2048], P('dp')
- first_gain_grad: float32 [2048], replicated
- first_shift_grad: float32 [2048], replicated
- mixing_weight_grad: float32 [2048, 3, 2048], P(None, None, 'tensor')
- mixing_bias_grad: float32 [2, 2048], P(None, 'tensor')
- output_weight_grad: float32 [2048, 2048], P('tensor')
- output_bias_grad: float32 [2048], replicated
- second_gain_grad: float32 [2048], replicated
- second_shift_grad: float32 [2048], replicated
- expand_weight_grad: float32 [2048, 8192], P(None, 'tensor')
- expand_bias_grad: float32 [8192], P('tensor')
- shrink_weight_grad: float32 [8192, 2048], P('tensor')
- shrink_bias_grad: float32 [2048], replicated
Inputs may be any that keep to these rules, and one draw needn't show every extreme that they name: `block_ids`: each sequence's block numbers start at 0, never fall, rise by one from block to block, give 4 blocks of 1 to 256 tokens, and one block has exactly 256 tokens.
All inputs are finite; a program needn't handle non-finite values.
Results may differ from a plain program's by a relative error of at most 0.014.
Values may be sent and summed in bfloat16 or wider, within the bound.
A program may use at most 256 MiB of HBM per device.

v0:
```python
import math
import jax
import jax.numpy as jnp
from jax import lax
from jax.sharding import PartitionSpec as P

H = 32
HD = 64
EPS = 1e-05


def layer_norm(values, scale_gain, shift_bias):
    row_mean = jnp.mean(values, axis=-1, keepdims=True)
    centred = values - row_mean
    row_var = jnp.mean(centred * centred, axis=-1, keepdims=True)
    return centred * lax.rsqrt(row_var + EPS) * scale_gain + shift_bias


def norm_backward(values, scale_gain, shift_bias, upstream):
    _, pull_back = jax.vjp(layer_norm, values, scale_gain, shift_bias)
    return pull_back(upstream)


def gelu_exact(values):
    return jax.nn.gelu(values, approximate=False)


def biased_scores(query, keys, blocks, first_head):
    length, local_heads, head_width = query.shape
    scores = jnp.einsum("qhd,khd->hqk", query, keys, preferred_element_type=jnp.float32) * (
        1.0 / math.sqrt(head_width)
    )
    heads_index = (first_head + jnp.arange(local_heads)).astype(jnp.float32)
    slopes = 2.0 ** (-8.0 * (heads_index + 1.0) / H)
    places = jnp.arange(length)
    offsets = (places[None, :] - places[:, None]).astype(jnp.float32)
    scores = scores + slopes[:, None, None] * offsets[None]
    allowed = blocks[None, :] <= blocks[:, None]
    return jnp.where(allowed[None], scores, -1e30)


def on_device(
    inputs,
    block_ids,
    first_gain,
    first_shift,
    mixing_weight,
    mixing_bias,
    output_weight,
    output_bias,
    second_gain,
    second_shift,
    expand_weight,
    expand_bias,
    shrink_weight,
    shrink_bias,
    cotangent,
):
    source = inputs.astype(jnp.float32)
    upstream = cotangent.astype(jnp.float32)
    length, width = source.shape
    blocks = block_ids[0]
    local_width = mixing_weight.shape[2]
    local_heads = local_width // HD
    first_head = lax.axis_index("tensor") * local_heads
    normed_low = layer_norm(source, first_gain, first_shift).astype(jnp.bfloat16)
    flat_weight = mixing_weight.reshape(width, 3 * local_width)
    mixed = jnp.dot(normed_low, flat_weight, preferred_element_type=jnp.float32).reshape(
        length, 3, local_width
    )
    query = (mixed[:, 0] + mixing_bias[0]).astype(jnp.bfloat16).reshape(length, local_heads, HD)
    keys = mixed[:, 1].astype(jnp.bfloat16).reshape(length, local_heads, HD)
    vals = (mixed[:, 2] + mixing_bias[1]).astype(jnp.bfloat16).reshape(length, local_heads, HD)
    masked = biased_scores(query, keys, blocks, first_head)
    row_top = jnp.max(masked, axis=-1, keepdims=True)
    logsum = row_top + jnp.log(jnp.sum(jnp.exp(masked - row_top), axis=-1, keepdims=True))
    probs_low = jnp.exp(masked - logsum).astype(jnp.bfloat16)
    attended = (
        jnp.einsum("hqk,khd->qhd", probs_low, vals, preferred_element_type=jnp.float32)
        .reshape(length, local_width)
        .astype(jnp.bfloat16)
    )
    partial_out = jnp.dot(attended, output_weight, preferred_element_type=jnp.float32)
    resid = lax.psum(partial_out, "tensor") + output_bias
    hidden_state = source + resid
    second_low = layer_norm(hidden_state, second_gain, second_shift).astype(jnp.bfloat16)
    pre_act = jnp.dot(second_low, expand_weight, preferred_element_type=jnp.float32) + expand_bias
    activ_low = gelu_exact(pre_act).astype(jnp.bfloat16)
    partial_mlp = jnp.dot(activ_low, shrink_weight, preferred_element_type=jnp.float32)
    outputs = (
        hidden_state
        + lax.psum(partial_mlp.astype(jnp.bfloat16), "tensor").astype(jnp.float32)
        + shrink_bias
    ).astype(jnp.bfloat16)
    act_grad = jnp.einsum("td,fd->tf", cotangent, shrink_weight, preferred_element_type=jnp.float32)
    _, gelu_pull = jax.vjp(gelu_exact, pre_act)
    pre_grad = gelu_pull(act_grad)[0].astype(jnp.bfloat16)
    shrink_weight_grad = jnp.einsum(
        "tf,td->fd", activ_low, cotangent, preferred_element_type=jnp.float32
    )
    shrink_bias_grad = jnp.sum(upstream, axis=0)
    expand_weight_grad = jnp.einsum(
        "td,tf->df", second_low, pre_grad, preferred_element_type=jnp.float32
    )
    expand_bias_grad = jnp.sum(pre_grad.astype(jnp.float32), axis=0)
    second_part = jnp.einsum(
        "tf,df->td", pre_grad, expand_weight, preferred_element_type=jnp.float32
    )
    second_grad = lax.psum(second_part, "tensor")
    hidden_grad, second_gain_grad, second_shift_grad = norm_backward(
        hidden_state, second_gain, second_shift, second_grad
    )
    hidden_grad = hidden_grad + upstream
    resid_low = hidden_grad.astype(jnp.bfloat16)
    output_weight_grad = jnp.einsum(
        "tc,td->cd", attended, resid_low, preferred_element_type=jnp.float32
    )
    output_bias_grad = jnp.sum(resid_low.astype(jnp.float32), axis=0)
    attended_grad = (
        jnp.einsum("td,cd->tc", resid_low, output_weight, preferred_element_type=jnp.float32)
        .astype(jnp.bfloat16)
        .reshape(length, local_heads, HD)
    )
    probs = jnp.exp(biased_scores(query, keys, blocks, first_head) - logsum)
    probs_low = probs.astype(jnp.bfloat16)
    prob_grad = jnp.einsum("qhd,khd->hqk", attended_grad, vals, preferred_element_type=jnp.float32)
    vals_grad = jnp.einsum(
        "hqk,qhd->khd", probs_low, attended_grad, preferred_element_type=jnp.float32
    ).astype(jnp.bfloat16)
    row_delta = jnp.sum(probs * prob_grad, axis=-1, keepdims=True)
    score_grad = (probs * (prob_grad - row_delta)).astype(jnp.bfloat16)
    scale_factor = 1.0 / math.sqrt(HD)
    query_grad = (
        jnp.einsum("hqk,khd->qhd", score_grad, keys, preferred_element_type=jnp.float32)
        * scale_factor
    ).astype(jnp.bfloat16)
    keys_grad = (
        jnp.einsum("hqk,qhd->khd", score_grad, query, preferred_element_type=jnp.float32)
        * scale_factor
    ).astype(jnp.bfloat16)
    mixed_grad = jnp.stack([query_grad, keys_grad, vals_grad], axis=1).reshape(
        length, 3 * local_width
    )
    mixing_weight_grad = jnp.einsum(
        "td,tc->dc", normed_low, mixed_grad, preferred_element_type=jnp.float32
    ).reshape(width, 3, local_width)
    mixing_bias_grad = jnp.stack(
        [
            jnp.sum(query_grad.astype(jnp.float32), axis=0).reshape(local_width),
            jnp.sum(vals_grad.astype(jnp.float32), axis=0).reshape(local_width),
        ]
    )
    normed_part = jnp.einsum(
        "tc,dc->td", mixed_grad, flat_weight, preferred_element_type=jnp.float32
    )
    normed_grad = lax.psum(normed_part, "tensor")
    source_grad, first_gain_grad, first_shift_grad = norm_backward(
        source, first_gain, first_shift, normed_grad
    )
    input_grad = (source_grad + hidden_grad).astype(jnp.bfloat16)
    summed = lax.psum(
        (
            first_gain_grad,
            first_shift_grad,
            mixing_weight_grad,
            mixing_bias_grad,
            output_weight_grad,
            output_bias_grad,
            second_gain_grad,
            second_shift_grad,
            expand_weight_grad,
            expand_bias_grad,
            shrink_weight_grad,
            shrink_bias_grad,
        ),
        "dp",
    )
    return (
        outputs,
        input_grad,
        summed[0],
        summed[1],
        summed[2],
        summed[3],
        summed[4],
        summed[5],
        summed[6],
        summed[7],
        summed[8],
        summed[9],
        summed[10],
        summed[11],
    )


def solution(mesh):
    in_specs = (
        P("dp", None),
        P("dp", None),
        P(),
        P(),
        P(None, None, "tensor"),
        P(None, "tensor"),
        P("tensor", None),
        P(),
        P(),
        P(),
        P(None, "tensor"),
        P("tensor"),
        P("tensor", None),
        P(),
        P("dp", None),
    )
    out_specs = (
        P("dp", None),
        P("dp", None),
        P(),
        P(),
        P(None, None, "tensor"),
        P(None, "tensor"),
        P("tensor", None),
        P(),
        P(),
        P(),
        P(None, "tensor"),
        P("tensor"),
        P("tensor", None),
        P(),
    )
    return jax.shard_map(
        on_device, mesh=mesh, in_specs=in_specs, out_specs=out_specs, check_vma=False
    )
```

profile of v0, /device:TPU:0, one launch (start us, length us, event | category | flops | bytes accessed | tf_op | source)
XLA Modules:
  0.0 1608.9 jit_solution(12495282931637150068)
XLA Ops:
  13.2 8.8 copy.34
  22.0 8.5 fusion.13
  33.1 11.5 fusion.48
  44.6 8.9 exponential_reduce_fusion
  53.5 9.8 fusion.26
  68.8 225.7 %all-reduce.8.cloned.1.call-done = f32[768,2048]{1,0:T(8,128)} async-done(((f32[768,2048]{1,0:T(8,128)}), f32[768,2048]{1,0:T(8,128)}) %all-reduce.8.cloned.1.call-update) | async-done | bytes 6291472 | tf_op jit(solution)/shard_map/psum | solution.py:84
  299.9 11.6 fusion.41
  311.5 26.1 %convert_reduce_fusion.2 = (f32[2048]{0:T(1024)}, bf16[768,2048]{1,0:T(8,128)(2,1)S(1)}, f32[768,2048]{1,0:T(8,128)}) fusion(f32[768,2048]{1,0:T(8,128)S(1)} %fusion.41, f32[2048]{0:T(1024)S(1)} %copy-done.37, bf16[768,2048]{1,0:T(8,128)(2,1)S(1)} %copy-done.9, bf16[2048,2048]{1,0:T(8,128)(2,1)} %param.27), kind=kOutput, calls=%fused_computation.28 | convolution fusion | flops 6560413696 | bytes 27279360 | tf_op jit(solution)/shard_map/td,fd->tf/dot_general | solution.py:95
  339.3 10.9 fusion.50
  358.8 10.2 convolution_convert_fusion
  369.1 203.1 %all-reduce.12.cloned.1.call-done = f32[768,2048]{1,0:T(8,128)} async-done(((f32[768,2048]{1,0:T(8,128)}), f32[768,2048]{1,0:T(8,128)}) %all-reduce.12.cloned.1.call-update) | async-done | bytes 6291472 | tf_op jit(solution)/shard_map/psum | solution.py:109
  578.0 117.2 %all-reduce.10.cloned.1.call-done = bf16[768,2048]{1,0:T(8,128)(2,1)} async-done(((bf16[768,2048]{1,0:T(8,128)(2,1)}), bf16[768,2048]{1,0:T(8,128)(2,1)}) %all-reduce.10.cloned.1.call-update) | async-done | bytes 3145744 | tf_op jit(solution)/shard_map/psum | solution.py:92
  695.2 8.1 fusion.45
  707.8 9.6 convert_reduce_fusion.4
  717.4 11.9 multiply_reduce_fusion
  729.3 13.7 multiply_convert_fusion
  756.8 12.9 fusion.53
  769.7 14.0 fusion.40
  787.6 9.8 fusion.33
  797.6 181.1 %all-reduce.14.cloned.1.call-done = f32[768,2048]{1,0:T(8,128)} async-done(((f32[768,2048]{1,0:T(8,128)}), f32[768,2048]{1,0:T(8,128)}) %all-reduce.14.cloned.1.call-update) | async-done | bytes 6291472 | tf_op jit(solution)/shard_map/psum | solution.py:156
  995.5 27.8 %all-reduce = (f32[2048]{0:T(1024)}, f32[2048]{0:T(1024)}, f32[2,512]{1,0:T(2,128)}, f32[2048]{0:T(1024)}, f32[2048]{0:T(1024)}, /*index=5*/f32[2048]{0:T(1024)}, f32[2048]{0:T(1024)}, f32[2048]{0:T(1024)}) all-reduce(f32[2048]{0:T(1024)S(1)} %get-tuple-element.16, ...), channel_id=1, replica_groups=mesh['dp'=8,'tensor'=4] {'dp'}, use_global_device_ids=true, to_apply=%region_16.17 | all-reduce | flops 15360 | bytes 122880 | tf_op jit(solution)/shard_map/psum | solution.py:161
  1023.4 543.2 %all-reduce.16.cloned.1.call-done = (f32[2048,3,512]{2,0,1:T(8,128)}, f32[512,2048]{1,0:T(8,128)}, f32[2048,2048]{1,0:T(8,128)}, f32[2048,2048]{1,0:T(8,128)}) async-done(((f32[2048,3,512]{2,0,1:T(8,128)}, f32[512,2048]{1,0:T(8,128)}, f32[2048,2048]{1,0:T(8,128)}, f32[2048,2048]{1,0:T(8,128)}), (f32[2048,3,512]{2,0,1:T(8,128)}, f32[512,2048]{1,0:T(8,128)}, f32[2048,2048]{1,0:T(8,128)}, ...) | async-done | bytes 50331664 | tf_op jit(solution)/shard_map/psum | solution.py:161
  1566.6 11.1 copy.54
  1579.8 14.0 copy.56
  (162 shorter events, 84.8 us)
Async XLA Ops:
  7.2 57.0 %copy-start = (bf16[512,2048]{1,0:T(8,128)(2,1)S(1)}, bf16[512,2048]{1,0:T(8,128)(2,1)}, u32[]{:S(2)}) copy-start(bf16[512,2048]{1,0:T(8,128)(2,1)} %param.21) | copy-start | bytes 6291460
  7.2 287.3 %all-reduce.8.cloned.1.call-start = ((), (), s32[]{:S(2)}) async-start(), calls=%async_computation | async-start | bytes 12582912 | tf_op jit(solution)/shard_map/psum | solution.py:84
  30.6 14.0 copy-start.15
  32.6 20.9 %copy-start.30 = (f32[8,64]{1,0:T(8,128)}, f32[8,64]{1,0:T(8,128)S(1)}, u32[]{:S(2)}) copy-start(f32[8,64]{1,0:T(8,128)S(1)} %add.163) | copy-start | bytes 6148
  32.7 11.9 copy-start.35
  64.2 230.3 %copy-start.38 = (f32[2048]{0:T(1024)S(1)}, f32[2048]{0:T(1024)}, u32[]{:S(2)}) copy-start(f32[2048]{0:T(1024)} %param.22) | copy-start | bytes 24580
  68.8 503.4 %all-reduce.12.cloned.1.call-start = ((), (), s32[]{:S(2)}) async-start(), calls=%async_computation.2 | async-start | bytes 12582912 | tf_op jit(solution)/shard_map/psum | solution.py:109
  299.1 12.4 copy-start.5
  311.5 26.1 %copy-start.12 = (f32[768,2048]{1,0:T(8,128)}, f32[768,2048]{1,0:T(8,128)S(1)}, u32[]{:S(2)}) copy-start(f32[768,2048]{1,0:T(8,128)S(1)} %fusion.41) | copy-start | bytes 18874372
  350.3 345.0 %all-reduce.10.cloned.1.call-start = ((), (), s32[]{:S(2)}) async-start(), calls=%async_computation.1 | async-start | bytes 6291456 | tf_op jit(solution)/shard_map/psum | solution.py:92
  369.0 326.2 %copy-start.39 = (f32[2048]{0:T(1024)S(1)}, f32[2048]{0:T(1024)}, u32[]{:S(2)}) copy-start(f32[2048]{0:T(1024)} %param.28) | copy-start | bytes 24580
  369.0 609.6 %all-reduce.14.cloned.1.call-start = ((), (), s32[]{:S(2)}) async-start(), calls=%async_computation.3 | async-start | bytes 12582912 | tf_op jit(solution)/shard_map/psum | solution.py:156
  729.3 13.7 copy-start.13
  729.3 13.7 copy-start.36
  756.7 13.0 copy-start.44
  756.7 809.9 %all-reduce.16.cloned.1.call-start = ((), (), s32[]{:S(2)}) async-start(), calls=%async_computation.4 | async-start | bytes 100663296 | tf_op jit(solution)/shard_map/psum | solution.py:161
  756.8 12.9 copy-start.48
  769.7 14.0 copy-start.18
  769.7 14.0 copy-start.21
  797.4 186.2 %copy-start.33 = (f32[768]{0:T(1024)S(1)}, f32[768]{0:T(1024)}, u32[]{:S(2)}) copy-start(f32[768]{0:T(1024)} %copy-done.32) | copy-start | bytes 9220
  1577.7 16.2 %slice-start = ((s8[16777216]{0:T(1024)(128)(4,1)}), s8[4194304]{0:T(1024)(128)(4,1)S(1)}, s32[]{:S(2)}) async-start(s8[16777216]{0:T(1024)(128)(4,1)} %bitcast.61), calls=%async_computation.5 | async-start | bytes 8388608
  1579.8 14.0 slice-start.1
  1579.8 14.0 slice-start.2
  1579.8 16.0 slice-start.3
  (36 other events, 194.1 us)
Sparse Core Ops, SparseCore 0:
  68.9 225.5 all-reduce.7
  350.4 221.7 all-reduce.11
  575.2 120.0 all-reduce.9
  756.8 221.8 all-reduce.13
  983.9 582.6 all-reduce.15
where the time goes:
time: 1620 us; the launch traced here: 1610 us
  waiting for transfers between devices  1270 us (78%)
  matrix products  169 us (10%)
  other arithmetic  71.5 us (4%)
  local copies, waits for them, and re-layouts  55.2 us (3%)
  blocking collectives  27.8 us (2%)
    psum x1, waiting for transfers between devices, on_device(): lax.psum((first_gain_grad, first_shift_grad, mixing_weight_grad, mixing_b...  543 us
    psum x1, waiting for transfers between devices, on_device(): resid = lax.psum(partial_out, 'tensor') + output_bias  226 us
    psum x1, waiting for transfers between devices, on_device(): second_grad = lax.psum(second_part, 'tensor')  203 us
    psum x1, waiting for transfers between devices, on_device(): normed_grad = lax.psum(normed_part, 'tensor')  181 us
    psum x1, waiting for transfers between devices, on_device(): lax.psum(partial_mlp.astype(jnp.bfloat16), 'tensor').astype(jnp.float32)  117 us
    unnamed x115, local copies, waits for them, and re-layouts  53 us
  transfers between devices with their start and end apart: 5, of which 5 were waited for; matrix products, arithmetic and copies ran while one was open for 5% of the time, Pallas kernels for 0%

commit v1 on v0

--- a/solution.py
+++ b/solution.py
@@ -7,6 +7,14 @@
 H = 32
 HD = 64
 EPS = 1e-05
+
+
+def add_in_pairs(x, name):
+    peers, result = (lax.axis_size(name), x)
+    for far in [1 << k for k in range(peers.bit_length() - 1)]:
+        swap = [(i, i ^ far) for i in range(peers)]
+        result = result + lax.ppermute(result, name, swap)
+    return result
 
 
 def layer_norm(values, scale_gain, shift_bias):
@@ -106,7 +114,7 @@
     second_part = jnp.einsum(
         "tf,df->td", pre_grad, expand_weight, preferred_element_type=jnp.float32
     )
-    second_grad = lax.psum(second_part, "tensor")
+    second_grad = add_in_pairs(second_part, "tensor")
     hidden_grad, second_gain_grad, second_shift_grad = norm_backward(
         hidden_state, second_gain, second_shift, second_grad
     )

time: 1620 us -> 1800 us (1.11)
  waiting for transfers between devices: 1270 us -> 1450 us
    ppermute x0 -> x2, waiting for transfers between devices: none -> 496 us  [add_in_pairs(): result = result + lax.ppermute(result, name, swap)]
    psum x1 -> x0, waiting for transfers between devices: 203 us -> none  [on_device(): second_grad = lax.psum(second_part, 'tensor')]
    psum x1, waiting for transfers between devices: 117 us -> 0.02 us  [on_device(): lax.psum(partial_mlp.astype(jnp.bfloat16), 'tensor').astype(jnp.float32)]
    unnamed x115 -> x119, local copies, waits for them, and re-layouts: 53 us -> 54 us
  transfers between devices with their start and end apart: 5 -> 6, of which waited for: 5 -> 5; matrix products, arithmetic and copies ran while one was open for 5% -> 4% of each run, Pallas kernels for 0% -> 0%
where the time goes in v1:
time: 1800 us; the launch traced here: 1790 us
  waiting for transfers between devices  1450 us (81%)
  matrix products  166 us (9%)
  other arithmetic  80.2 us (4%)
  local copies, waits for them, and re-layouts  56.3 us (3%)
  blocking collectives  27.8 us (2%)
    psum x1, waiting for transfers between devices, on_device(): lax.psum((first_gain_grad, first_shift_grad, mixing_weight_grad, mixing_b...  543 us
    ppermute x2, waiting for transfers between devices, add_in_pairs(): result = result + lax.ppermute(result, name, swap)  496 us
    psum x1, waiting for transfers between devices, on_device(): resid = lax.psum(partial_out, 'tensor') + output_bias  226 us
    psum x1, waiting for transfers between devices, on_device(): normed_grad = lax.psum(normed_part, 'tensor')  181 us
    unnamed x119, local copies, waits for them, and re-layouts  54 us
  transfers between devices with their start and end apart: 6, of which 5 were waited for; matrix products, arithmetic and copies ran while one was open for 4% of the time, Pallas kernels for 0%

profile of v1, /device:TPU:0, one launch (start us, length us, event | category | flops | bytes accessed | tf_op | source)
XLA Modules:
  0.0 1793.0 jit_solution(2444355581585543931)
XLA Ops:
  13.2 8.8 copy.34
  33.1 11.5 fusion.48
  44.6 8.9 exponential_reduce_fusion
  53.5 9.9 fusion.26
  68.9 225.7 %all-reduce.7.cloned.1.call-done = f32[768,2048]{1,0:T(8,128)} async-done(((f32[768,2048]{1,0:T(8,128)}), f32[768,2048]{1,0:T(8,128)}) %all-reduce.7.cloned.1.call-update) | async-done | bytes 6291472 | tf_op jit(solution)/shard_map/psum | solution.py:92
  300.0 11.6 fusion.41
  311.6 23.3 %convert_reduce_fusion.2 = (f32[2048]{0:T(1024)}, bf16[768,2048]{1,0:T(8,128)(2,1)S(1)}, f32[768,2048]{1,0:T(8,128)S(1)}) fusion(f32[768,2048]{1,0:T(8,128)S(1)} %fusion.41, f32[2048]{0:T(1024)S(1)} %copy-done.39, bf16[768,2048]{1,0:T(8,128)(2,1)S(1)} %copy-done.9, bf16[2048,2048]{1,0:T(8,128)(2,1)} %param.27), kind=kOutput, calls=%fused_computation.28 | convolution fusion | flops 6560413696 | bytes 27279360 | tf_op jit(solution)/shard_map/td,fd->tf/dot_general | solution.py:103
  334.9 10.2 fusion.50
  347.9 137.4 %collective-permute-done = f32[768,2048]{1,0:T(8,128)} collective-permute-done((f32[768,2048]{1,0:T(8,128)S(1)}, f32[768,2048]{1,0:T(8,128)}, u32[]{:S(2)}, u32[]{:S(2)}) %collective-permute-start) | collective-permute-done | bytes 6291488 | tf_op jit(solution)/shard_map/ppermute | solution.py:16
  485.2 9.2 add.189
  499.1 10.4 convolution_convert_fusion
  509.6 359.1 %collective-permute-done.1 = f32[768,2048]{1,0:T(8,128)} collective-permute-done((f32[768,2048]{1,0:T(8,128)}, f32[768,2048]{1,0:T(8,128)}, u32[]{:S(2)}, u32[]{:S(2)}) %collective-permute-start.1) | collective-permute-done | bytes 6291488 | tf_op jit(solution)/shard_map/ppermute | solution.py:16
  868.7 10.2 multiply_reduce_fusion.1
  891.6 9.6 convert_reduce_fusion.4
  901.2 11.9 multiply_reduce_fusion
  913.1 13.7 multiply_convert_fusion
  940.6 12.9 fusion.53
  953.5 14.0 fusion.40
  971.4 9.8 fusion.33
  981.4 181.5 %all-reduce.11.cloned.1.call-done = f32[768,2048]{1,0:T(8,128)} async-done(((f32[768,2048]{1,0:T(8,128)}), f32[768,2048]{1,0:T(8,128)}) %all-reduce.11.cloned.1.call-update) | async-done | bytes 6291472 | tf_op jit(solution)/shard_map/psum | solution.py:164
  1179.7 27.8 %all-reduce = (f32[2048]{0:T(1024)}, f32[2048]{0:T(1024)}, f32[2,512]{1,0:T(2,128)}, f32[2048]{0:T(1024)}, f32[2048]{0:T(1024)}, /*index=5*/f32[2048]{0:T(1024)}, f32[2048]{0:T(1024)}, f32[2048]{0:T(1024)}) all-reduce(f32[2048]{0:T(1024)S(1)} %get-tuple-element.16, ...), channel_id=1, replica_groups=mesh['dp'=8,'tensor'=4] {'dp'}, use_global_device_ids=true, to_apply=%region_15.16 | all-reduce | flops 15360 | bytes 122880 | tf_op jit(solution)/shard_map/psum | solution.py:169
  1207.5 543.2 %all-reduce.13.cloned.1.call-done = (f32[2048,3,512]{2,0,1:T(8,128)}, f32[512,2048]{1,0:T(8,128)}, f32[2048,2048]{1,0:T(8,128)}, f32[2048,2048]{1,0:T(8,128)}) async-done(((f32[2048,3,512]{2,0,1:T(8,128)}, f32[512,2048]{1,0:T(8,128)}, f32[2048,2048]{1,0:T(8,128)}, f32[2048,2048]{1,0:T(8,128)}), (f32[2048,3,512]{2,0,1:T(8,128)}, f32[512,2048]{1,0:T(8,128)}, f32[2048,2048]{1,0:T(8,128)}, ...) | async-done | bytes 50331664 | tf_op jit(solution)/shard_map/psum | solution.py:169
  1750.8 11.1 copy.53
  1764.0 14.0 copy.55
  (168 shorter events, 92.9 us)
Async XLA Ops:
  7.2 57.1 %copy-start = (bf16[512,2048]{1,0:T(8,128)(2,1)S(1)}, bf16[512,2048]{1,0:T(8,128)(2,1)}, u32[]{:S(2)}) copy-start(bf16[512,2048]{1,0:T(8,128)(2,1)} %param.21) | copy-start | bytes 6291460
  7.2 287.4 %all-reduce.7.cloned.1.call-start = ((), (), s32[]{:S(2)}) async-start(), calls=%async_computation | async-start | bytes 12582912 | tf_op jit(solution)/shard_map/psum | solution.py:92
  30.6 14.0 copy-start.15
  32.6 20.9 %copy-start.32 = (f32[8,64]{1,0:T(8,128)}, f32[8,64]{1,0:T(8,128)S(1)}, u32[]{:S(2)}) copy-start(f32[8,64]{1,0:T(8,128)S(1)} %add.167) | copy-start | bytes 6148
  32.7 11.9 copy-start.37
  64.3 230.3 %copy-start.40 = (f32[2048]{0:T(1024)S(1)}, f32[2048]{0:T(1024)}, u32[]{:S(2)}) copy-start(f32[2048]{0:T(1024)} %param.22) | copy-start | bytes 24580
  68.9 810.1 %all-reduce.9.cloned.1.call-start = ((), (), s32[]{:S(2)}) async-start(), calls=%async_computation.1 | async-start | bytes 6291456 | tf_op jit(solution)/shard_map/psum | solution.py:100
  299.2 12.5 copy-start.5
  347.9 137.4 %collective-permute-start = (f32[768,2048]{1,0:T(8,128)S(1)}, f32[768,2048]{1,0:T(8,128)}, u32[]{:S(2)}, u32[]{:S(2)}) collective-permute-start(f32[768,2048]{1,0:T(8,128)S(1)} %fusion.50), channel_id=1, source_target_pairs={{0,1},{1,0},{2,3},{3,2},{4,5},{5,4},{6,7},{7,6},{8,9},{9,8},{10,11... | collective-permute-start | bytes 18874376 | tf_op jit(solution)/shard_map/ppermute | solution.py:16
  494.5 374.2 %collective-permute-start.1 = (f32[768,2048]{1,0:T(8,128)}, f32[768,2048]{1,0:T(8,128)}, u32[]{:S(2)}, u32[]{:S(2)}) collective-permute-start(f32[768,2048]{1,0:T(8,128)} %add.189), channel_id=1, source_target_pairs={{0,2},{1,3},{2,0},{3,1},{4,6},{5,7},{6,4},{7,5},{8,10},{9,11},{10,... | collective-permute-start | bytes 18874376 | tf_op jit(solution)/shard_map/ppermute | solution.py:16
  509.5 369.5 %copy-start.41 = (f32[2048]{0:T(1024)S(1)}, f32[2048]{0:T(1024)}, u32[]{:S(2)}) copy-start(f32[2048]{0:T(1024)} %param.28) | copy-start | bytes 24580
  509.5 653.3 %all-reduce.11.cloned.1.call-start = ((), (), s32[]{:S(2)}) async-start(), calls=%async_computation.2 | async-start | bytes 12582912 | tf_op jit(solution)/shard_map/psum | solution.py:164
  913.1 13.7 copy-start.13
  913.1 13.7 copy-start.38
  940.5 13.0 copy-start.46
  940.5 810.2 %all-reduce.13.cloned.1.call-start = ((), (), s32[]{:S(2)}) async-start(), calls=%async_computation.3 | async-start | bytes 100663296 | tf_op jit(solution)/shard_map/psum | solution.py:169
  940.6 12.9 copy-start.50
  953.5 14.0 copy-start.18
  953.5 14.0 copy-start.21
  981.2 186.5 %copy-start.35 = (f32[768]{0:T(1024)S(1)}, f32[768]{0:T(1024)}, u32[]{:S(2)}) copy-start(f32[768]{0:T(1024)} %copy-done.34) | copy-start | bytes 9220
  1761.8 16.2 slice-start
  1763.9 14.0 slice-start.1
  1764.0 14.0 slice-start.2
  1764.0 16.0 slice-start.3
  (39 other events, 217.3 us)
Sparse Core Ops, SparseCore 0:
  69.0 225.5 all-reduce.6
  509.6 286.1 all-reduce.8
  940.6 222.1 all-reduce.10
  1168.1 582.6 all-reduce.12
